TPU v7x, 32 devices: a whole 2x2x4 slice. The times are simulated.
32 devices in a mesh: row: 4 (over z), col: 8 (over y, x, core).
Axes of the slice: x: 2, y: 2, z: 4, core: 2. Of those that a mesh axis runs over, the one named last changes fastest.
Arguments:
- species: float32 [53, 32, 64, 256], P(None, 'row', 'col'), may hold values from 0.05 to 2
- velocity: float32 [3, 32, 64, 256], P(None, 'row', 'col'), may hold values from -1 to 1
- diffusivity: float32 [53], replicated, may hold values from 0.02 to 0.1
- divergence: float32 [32, 64, 256], P('row', 'col'), may hold values from -6 to 6
- log_rates: float32 [325], replicated, may hold values from -3 to 1
- reactants: int32 [325, 53], replicated, may hold values from 0 to 3, as said below
- products: int32 [325, 53], replicated, may hold values from 0 to 3, as said below
- heat_weights: float32 [53], replicated, may hold values from -0.875 to 0.875
- substeps: int32 [32, 64, 2], P('row', 'col'), may hold values from 1 to 6
Outputs:
- reacted: float32 [53, 32, 64, 256], P(None, 'row', 'col')
- pressure: float32 [32, 64, 256], P('row', 'col')
Inputs may be any that keep to these rules, and one draw needn't show every extreme that they name: `reactants`: each reaction has one or two reactant species. `products`: each reaction has one or two product species.
All inputs are finite; a program needn't handle non-finite values.
Results may differ from a plain program's by a relative error of at most 0.0003.
Values sent between devices are 32-bit elements; how exact they have to be, the bound alone decides.
No kernel may reach another device: no remote copies, remote signals or barrier semaphores. Data moves between devices by JAX's collectives and lax.ppermute only.
A program may use at most 128 MiB of HBM per device.

v0:
```python
import functools
import math

import jax
import jax.numpy as jnp
import numpy as np
from jax import lax
from jax.experimental import pallas as pl
from jax.experimental.pallas import tpu as pltpu
from jax.sharding import PartitionSpec as P

BLOCK = 128
MAXSUB = 6
LANES = 128
TILE = 8

time_step = 0.2
screen = 0.004
log2e = 1.4426950408889634
f32 = jnp.float32
bf16 = jnp.bfloat16


def round_up(value, multiple):
    return -(-value // multiple) * multiple


def cosine_table(length):
    wave = np.arange(length, dtype=np.float64)
    weight = np.where(wave == 0, math.sqrt(1.0 / length), math.sqrt(2.0 / length))
    table = weight[:, None] * np.cos(math.pi * wave[:, None] * (wave[None, :] + 0.5) / length)
    return table.astype(np.float32)


def mode_values(length):
    wave = np.arange(length, dtype=np.float64)
    return 2.0 - 2.0 * np.cos(math.pi * wave / length)


def halves(value):
    high = value.astype(bf16)
    return high, (value - high.astype(f32)).astype(bf16)


def dot_halves(left, right, dims=((1,), (0,))):
    def product(a, b):
        return lax.dot_general(a, b, (dims, ((), ())), preferred_element_type=f32)

    small = product(left[1], right[0]) + product(left[0], right[1])
    return product(left[0], right[0]) + small


def dot3(left, right, dims=((1,), (0,))):
    return dot_halves(halves(left), halves(right), dims)


def transport_weights(velocity):
    ups = [time_step * jnp.maximum(v, 0.0) for v in velocity]
    downs = [-time_step * jnp.minimum(v, 0.0) for v in velocity]
    own = 1.0
    for weight in ups + downs:
        own = own - weight
    return ups, downs, own


def z_neighbours(tiles):
    lane = lax.broadcasted_iota(jnp.int32, (TILE, LANES), 1)
    up = [pltpu.roll(t, 1, 1) for t in tiles]
    down = [pltpu.roll(t, LANES - 1, 1) for t in tiles]
    minus, plus = [], []
    last = len(tiles) - 1
    for i, tile in enumerate(tiles):
        minus.append(jnp.where(lane == 0, tile if i == 0 else up[i - 1], up[i]))
        plus.append(jnp.where(lane == LANES - 1, tile if i == last else down[i + 1], down[i]))
    return minus, plus


def sort_blocks(substeps, codes, inner_first):
    blocks = substeps.shape[1]
    square = (blocks, blocks)
    key = jnp.broadcast_to(substeps + inner_first, square)
    key_down = key.T
    down = lax.broadcasted_iota(jnp.int32, square, 0)
    across = lax.broadcasted_iota(jnp.int32, square, 1)
    ahead = (key_down > key) | ((key_down == key) & (down < across))
    rank = jnp.sum(jnp.where(ahead, 1.0, 0.0), axis=0, keepdims=True)
    rank_down = jnp.broadcast_to(rank, square).T
    value_down = jnp.broadcast_to(codes * 8.0 + substeps, square).T
    chosen = jnp.where(rank_down == across.astype(f32), value_down, 0.0)
    return jnp.sum(chosen, axis=0, keepdims=True).astype(jnp.int32)


def react_blocks(first_block, total, group, refs, target_of):
    order, steps, mv, conc, rp_ref, st_ref, heat, weight_ref = refs
    ns8 = conc.shape[0]
    pieces = st_ref.shape[1] // 2
    rows = rp_ref.shape[0]
    width = group * LANES

    def spread(row):
        return pl.ds(row, ns8, stride=TILE)

    def one_group(g, carry):
        base = first_block + g * group
        values = [order[0, base + i] for i in range(group)]
        ns = [value & 7 for value in values]
        hs = [steps[n] for n in ns]
        places = []
        for value in values:
            code = value >> 3
            places.append(((code >> 4) & 15, code & 1, (code >> 1) & 7, code >> 9))
        for i, (plane, half, row, _) in enumerate(places):
            conc[:, i * LANES : (i + 1) * LANES] = mv[plane, half, spread(row), :]

        def one_level(level, inner):
            held = conc[...]
            logs = jnp.log(held) * log2e
            high = logs.astype(bf16).astype(f32)
            low = logs - high
            fill = jnp.zeros((rp_ref.shape[1] - 2 * ns8, width), f32)
            stacked = jnp.concatenate([high, low, fill], axis=0).astype(bf16)
            rates = jnp.exp2(jnp.dot(rp_ref[...], stacked, preferred_element_type=f32))
            first, second = halves(rates)
            gap = jnp.zeros((pieces - rows, width), bf16)
            both = jnp.concatenate([first, gap, second, gap], axis=0)
            sums = jnp.dot(st_ref[...], both, preferred_element_type=f32)
            for i in range(group):
                part = slice(i * LANES, (i + 1) * LANES)
                old = held[:, part]
                fresh = old * (old + hs[i] * sums[:ns8, part]) / (old + hs[i] * sums[ns8:, part])
                conc[:, part] = jnp.where(ns[i] > level, fresh, old)
            return inner

        lax.fori_loop(0, ns[0], one_level, 0)
        for i, (plane, half, row, column) in enumerate(places):
            new = conc[:, i * LANES : (i + 1) * LANES]
            change = (new - mv[plane, half, spread(row), :]) * weight_ref[...]
            heat[half, pl.ds(column, 1), :] = jnp.sum(change, axis=0, keepdims=True)
            to_plane, to_row = target_of(plane, row)
            mv[to_plane, half, spread(to_row), :] = new
        return carry

    lax.fori_loop(0, total // group, one_group, 0)


def over_species(ns, body, unroll=4):
    def step(i, carry):
        for j in range(unroll):
            body(i * unroll + j)
        return carry

    lax.fori_loop(0, ns // unroll, step, 0)
    for s in range(ns - ns % unroll, ns):
        body(s)


def prepare_kernel(
    dims,
    log_rates,
    substeps,
    species_hbm,
    velocity_hbm,
    diffusivity_hbm,
    reactants_hbm,
    products_hbm,
    weights_hbm,
    codes_hbm,
    sp,
    row_a,
    row_b,
    col_a,
    col_b,
    velocity,
    diffusivity,
    rp_ref,
    st_ref,
    weight_ref,
    order_row,
    build,
    reactants,
    products,
    heat_weights,
    codes,
    in_sem,
    small_sem,
):
    ns, cx, cy, halves_z = dims
    nr = log_rates.shape[1]
    ns8 = weight_ref.shape[0]

    def load(x, z):
        return pltpu.make_async_copy(
            species_hbm.at[:, x, :, pl.ds(z * LANES, LANES)], sp.at[z, :, x], in_sem.at[x, z]
        )

    small = [
        pltpu.make_async_copy(source, target, small_sem.at[i])
        for i, (source, target) in enumerate(
            (
                (reactants_hbm, reactants),
                (products_hbm, products),
                (weights_hbm, heat_weights),
                (codes_hbm, codes),
                (diffusivity_hbm, diffusivity),
                (velocity_hbm, velocity),
            )
        )
    ]
    for copy in small[:5]:
        copy.start()
    for x in range(cx):
        for z in range(halves_z):
            load(x, z).start()
    small[5].start()
    for copy in small[:5]:
        copy.wait()
    order_row[...] = sort_blocks(substeps[...].astype(f32), codes[0:1, :], codes[1:2, :])
    react = reactants[...].astype(f32)
    build[...] = jnp.zeros_like(build)
    build[0:ns, 0:nr] = react
    build[ns8 : ns8 + ns, 0:nr] = react
    rest = log_rates[...] * log2e
    for i in range(3):
        piece = rest.astype(bf16).astype(f32)
        build[ns + i : ns + i + 1, 0:nr] = piece
        rest = rest - piece
    rp_ref[...] = build[...].T[: rp_ref.shape[0]].astype(bf16)
    build[...] = jnp.zeros_like(build)
    build[0:ns, 0:nr] = products[...].astype(f32)
    build[ns8 : ns8 + ns, 0:nr] = react
    half = build[0 : 2 * ns8, :].astype(bf16)
    st_ref[...] = jnp.concatenate([half, half], axis=1)
    build[:, 0:LANES] = jnp.zeros((build.shape[0], LANES), f32)
    build[:, 0:ns] = jnp.broadcast_to(heat_weights[...], (build.shape[0], ns))
    weight_ref[...] = build[:, 0:LANES].T[:ns8]

    row_even = lax.rem(lax.axis_index("row"), 2) == 0
    col_even = lax.rem(lax.axis_index("col"), 2) == 0
    x_a = jnp.where(row_even, cx - 1, 0)
    y_a = jnp.where(col_even, cy - 1, 0)
    flat = sp.reshape(halves_z, ns * cx * cy, LANES)
    for x in range(cx):
        for z in range(halves_z):
            load(x, z).wait()

    def body(s):
        for z in range(halves_z):
            q = slice(z * LANES, (z + 1) * LANES)
            row_a[s, :, q] = sp[z, s, x_a]
            row_b[s, :, q] = sp[z, s, cx - 1 - x_a]
            col_a[s, :, q] = flat[z, pl.ds(s * cx * cy + y_a, cx, stride=cy), :]
            col_b[s, :, q] = flat[z, pl.ds(s * cx * cy + cy - 1 - y_a, cx, stride=cy), :]

    over_species(ns, body)
    small[5].wait()


def fill_steps(steps):
    steps[0] = 0.0
    for n in range(1, MAXSUB + 2):
        steps[n] = float(np.float32(time_step) / np.float32(n))


def inner_kernel(
    dims,
    total,
    group,
    order,
    diffusivity,
    sp,
    velocity,
    rp_ref,
    st_ref,
    weight_ref,
    mv,
    heat,
    conc,
    steps,
):
    ns, cx, cy, halves_z = dims
    ns8 = conc.shape[0]
    flat = sp.reshape(halves_z, ns * cx * cy, LANES)
    fill_steps(steps)
    mv[:, :, ns * TILE :, :] = jnp.full(
        (mv.shape[0], halves_z, (ns8 - ns) * TILE, LANES), 2.0, f32
    )
    heat[...] = jnp.zeros_like(heat)
    sublane = lax.broadcasted_iota(jnp.int32, (TILE, LANES), 0)

    def run_plane(slot, weights, tile_of):
        def body(s):
            d = time_step * diffusivity[0, s]
            got = [tile_of(s, z) for z in range(halves_z)]
            zm, zp = z_neighbours([g[0] for g in got])
            for z in range(halves_z):
                c = got[z][0]
                ups, downs, own = weights[z]
                sides = [*got[z][1:], zm[z], zp[z]]
                wanted = [ups[0], downs[0], ups[1], downs[1], ups[2], downs[2]]
                value = own * c
                near = -6.0 * c
                for w, t in zip(wanted, sides):
                    if t is None:
                        continue
                    value = value + w * t
                    near = near + t
                mv[slot, z, pl.ds(s * TILE, TILE), :] = value + d * near

        over_species(ns, body)

    lanes = [pl.ds(z * LANES, LANES) for z in range(halves_z)]
    for x in range(1, cx - 1):
        weights = [transport_weights([velocity[d, x, :, q] for d in range(3)]) for q in lanes]

        def tile_of(s, z, x=x):
            c = sp[z, s, x]
            return (
                c,
                sp[z, s, x - 1],
                sp[z, s, x + 1],
                pltpu.roll(c, 1, 0),
                pltpu.roll(c, TILE - 1, 0),
            )

        run_plane(x - 1, weights, tile_of)
    for slot, x, inward in ((cx - 2, 0, 1), (cx - 1, cx - 1, -1)):
        weights = []
        for q in lanes:
            ups, downs, own = transport_weights([velocity[d, x, :, q] for d in range(3)])
            weights.append((ups, downs, own))

        def tile_of(s, z, x=x, inward=inward):
            c = sp[z, s, x]
            inner = sp[z, s, x + inward]
            ym = jnp.where(sublane == 0, 0.0, pltpu.roll(c, 1, 0))
            yp = jnp.where(sublane == TILE - 1, 0.0, pltpu.roll(c, TILE - 1, 0))
            if inward > 0:
                return c, None, inner, ym, yp
            return c, inner, None, ym, yp

        run_plane(slot, weights, tile_of)
    for slot, y, inward in ((cx, 0, 1), (cx + 1, cy - 1, -1)):
        weights = []
        for q in lanes:
            rows = [
                jnp.concatenate([velocity[d, x, y : y + 1, q] for x in range(cx)], axis=0)
                for d in range(3)
            ]
            weights.append(transport_weights(rows))

        def tile_of(s, z, y=y, inward=inward):
            c = flat[z, pl.ds(s * cx * cy + y, cx, stride=cy), :]
            inner = flat[z, pl.ds(s * cx * cy + y + inward, cx, stride=cy), :]
            xm = pltpu.roll(c, 1, 0)
            xp = pltpu.roll(c, TILE - 1, 0)
            if inward > 0:
                return c, xm, xp, None, inner
            return c, xm, xp, inner, None

        run_plane(slot, weights, tile_of)
    refs = (order, steps, mv, conc, rp_ref, st_ref, heat, weight_ref)
    react_blocks(0, total, group, refs, lambda plane, row: (plane, row))


def outer_kernel(
    dims,
    first_block,
    total,
    group,
    rows_count,
    cols_count,
    order,
    diffusivity,
    velocity,
    divergence,
    mv_in,
    heat_inner,
    rp_ref,
    st_ref,
    weight_ref,
    table_z,
    row_sent_a,
    row_sent_b,
    col_sent_a,
    col_sent_b,
    row_got_a,
    row_got_b,
    col_got_a,
    col_got_b,
    reacted_hbm,
    forward,
    mv,
    table_high,
    table_low,
    halo,
    conc,
    heat,
    steps,
    halo_sem,
    out_sem,
):
    ns, cx, cy, halves_z = dims
    fill_steps(steps)
    row = lax.axis_index("row")
    col = lax.axis_index("col")
    lanes = [pl.ds(z * LANES, LANES) for z in range(halves_z)]

    def fetch(source, side):
        for z, q in enumerate(lanes):
            pltpu.make_async_copy(source.at[:, :, q], halo.at[side, z], halo_sem.at[side, z]).start()

    for axis, (at, count, sent, got) in enumerate(
        (
            (row, rows_count, (row_sent_a, row_sent_b), (row_got_a, row_got_b)),
            (col, cols_count, (col_sent_a, col_sent_b), (col_got_a, col_got_b)),
        )
    ):
        even = lax.rem(at, 2) == 0
        for side, wall, kinds in (
            (2 * axis, at == 0, (1, 0)),
            (2 * axis + 1, at == count - 1, (0, 1)),
        ):
            for parity, kind in zip((even, jnp.logical_not(even)), kinds):
                pl.when(parity & wall)(functools.partial(fetch, sent[kind], side))
                pl.when(parity & jnp.logical_not(wall))(
                    functools.partial(fetch, got[kind], side)
                )
    sublane = lax.broadcasted_iota(jnp.int32, (TILE, LANES), 0)
    at_low = jnp.where(sublane == 0, 1.0, 0.0)
    at_high = jnp.where(sublane == TILE - 1, 1.0, 0.0)
    heat[...] = heat_inner[...]

    def arrive(side):
        for z, q in enumerate(lanes):
            pltpu.make_async_copy(
                row_got_a.at[:, :, q], halo.at[side, z], halo_sem.at[side, z]
            ).wait()

    for side in range(4):
        arrive(side)
    base = cx - 2
    for slot, x, y in ((2, None, 0), (3, None, cy - 1), (0, 0, None), (1, cx - 1, None)):
        weights = []
        for q in lanes:
            if y is None:
                ups, downs, _ = transport_weights([velocity[d, x, :, q] for d in range(2)])
                low = jnp.where(sublane == 0, ups[1], 0.0)
                high = jnp.where(sublane == TILE - 1, downs[1], 0.0)
                weights.append((ups[0] if slot == 0 else downs[0], low, high))
            else:
                across = jnp.concatenate([velocity[1, i, y : y + 1, q] for i in range(cx)], axis=0)
                ups, downs, _ = transport_weights([across])
                weights.append((ups[0] if slot == 2 else downs[0],))

        def body(s, slot=slot, x=x, y=y, weights=weights):
            d = time_step * diffusivity[0, s]
            for z in range(halves_z):
                rows = pl.ds(s * TILE, TILE)
                value = mv[base + slot, z, rows, :] + (weights[z][0] + d) * halo[slot, z, s]
                if y is None:
                    below = jnp.broadcast_to(halo[2, z, s, x : x + 1, :], (TILE, LANES))
                    above = jnp.broadcast_to(halo[3, z, s, x : x + 1, :], (TILE, LANES))
                    value = value + (weights[z][1] + d * at_low) * below
                    value = value + (weights[z][2] + d * at_high) * above
                mv[base + slot, z, rows, :] = value

        over_species(ns, body)

    def target_of(plane, at_row):
        ours = plane < base + 2
        edge = jnp.where(plane == base + 2, 0, cy - 1)
        return jnp.where(ours, plane, at_row - 1), jnp.where(ours, at_row, edge)

    refs = (order, steps, mv, conc, rp_ref, st_ref, heat, weight_ref)
    react_blocks(first_block, total, group, refs, target_of)

    def save(x, z):
        plane = {0: base, cx - 1: base + 1}.get(x, x - 1)
        tiles = mv.reshape(cx + 2, halves_z, conc.shape[0], TILE, LANES)
        return pltpu.make_async_copy(
            tiles.at[plane, z, 0:ns], reacted_hbm.at[:, x, :, lanes[z]], out_sem.at[x, z]
        )

    for x in range(cx):
        for z in range(halves_z):
            save(x, z).start()
    heat_all = jnp.concatenate([heat[z] for z in range(halves_z)], axis=1)
    source = divergence[...] - heat_all / time_step
    table_high[...], table_low[...] = halves(table_z[...])
    result = dot_halves((table_high[...], table_low[...]), halves(source), ((1,), (1,)))
    forward[...] = jnp.zeros_like(forward)
    forward[:, 0 : cx * cy] = result
    for x in range(cx):
        for z in range(halves_z):
            save(x, z).wait()


def solve_kernel(dims, lam_z, planes, table_y, mix_x, base, out, wide, tall):
    rows_count, cols_count, depth, cx, cy = dims
    cells = cx * cy
    nb = base.shape[1]
    na = rows_count * cx
    device = lax.axis_index("row") * cols_count + lax.axis_index("col")
    group = rows_count * depth
    total = jnp.zeros((group, cx * nb), f32)
    for c in range(cols_count):
        wide[c] = jnp.zeros((cells, cx * nb), f32)
        for x in range(cx):
            wide[c, x * cy : (x + 1) * cy, x * nb : (x + 1) * nb] = table_y[c * cy : (c + 1) * cy, :]
        if planes.ndim == 2:
            block = jnp.concatenate(
                [
                    planes[(r * cols_count + c) * depth : (r * cols_count + c + 1) * depth, 0:cells]
                    for r in range(rows_count)
                ],
                axis=0,
            )
        else:
            block = planes[c, :, 0:cells]
        total = total + dot3(block, wide[c])
    for x in range(cx):
        tall[x * group : (x + 1) * group, :] = total[:, x * nb : (x + 1) * nb]
    spectrum = dot3(mix_x[...], tall[...])
    solved = []
    for k in range(depth):
        rows = slice(k * na, (k + 1) * na)
        solved.append(spectrum[rows] / (base[...] + lam_z[device * depth + k]))
    spectrum = jnp.concatenate(solved, axis=0)
    back = dot3(mix_x[...], spectrum, ((0,), (0,)))
    row = jnp.concatenate([back[x * group : (x + 1) * group] for x in range(cx)], axis=1)
    out[...] = jnp.zeros_like(out)
    for c in range(cols_count):
        block = dot3(row, wide[c], ((1,), (1,)))
        if planes.ndim == 2:
            for r in range(rows_count):
                at = (r * cols_count + c) * depth
                out[at : at + depth, 0:cells] = block[r * depth : (r + 1) * depth]
        else:
            out[c, :, 0:cells] = block


def inverse_kernel(columns, table_high, table_low, out):
    cells = out.shape[0]
    out[...] = dot_halves(halves(columns[...].T[:cells]), (table_high[...], table_low[...]))


smem = pl.BlockSpec(memory_space=pltpu.SMEM)
vmem = pl.BlockSpec(memory_space=pltpu.VMEM)
anywhere = pl.BlockSpec(memory_space=pl.ANY)
hbm = pl.BlockSpec(memory_space=pltpu.HBM)


def pick_group(total, most):
    best = 2
    for group in range(2, most + 1, 2):
        if total % group == 0:
            best = group
    return best


def local(
    species,
    velocity,
    diffusivity,
    divergence,
    log_rates,
    reactants,
    products,
    heat_weights,
    substeps,
):
    ns, cx, cy, nz = species.shape
    nr = log_rates.shape[0]
    rows_count = lax.axis_size("row")
    cols_count = lax.axis_size("col")
    device_count = rows_count * cols_count
    halves_z = nz // LANES
    ns8 = round_up(ns + 3, TILE)
    nr_rows = round_up(nr, 16)
    nr_lanes = round_up(nr, LANES)
    depth = nz // device_count
    cells = cx * cy
    dims = (ns, cx, cy, halves_z)

    codes = np.zeros((TILE, cells * halves_z), np.float32)
    inner_total = 0
    for x in range(cx):
        for y in range(cy):
            inside = 0 < x < cx - 1 and 0 < y < cy - 1
            if x in (0, cx - 1):
                slot, at = cx - 2 + (x > 0), y
            elif inside:
                slot, at = x - 1, y
            else:
                slot, at = cx + (y > 0), x
            for z in range(halves_z):
                flat = (x * cy + y) * halves_z + z
                codes[0, flat] = flat << 8 | slot << 4 | at << 1 | z
                codes[1, flat] = 8.0 * inside
                inner_total += inside
    outer_total = cells * halves_z - inner_total
    inner_group = pick_group(inner_total, 12)
    outer_group = pick_group(outer_total, 14)

    def array(*shape, dtype=f32):
        return jax.ShapeDtypeStruct(shape, dtype)

    mv_shape = (cx + 2, halves_z, ns8 * TILE, LANES)
    estimate = pl.CostEstimate(flops=10**10, bytes_accessed=10**7, transcendentals=10**7)
    sp, row_a, row_b, col_a, col_b, speed, spread, rp, st, weight, order = pl.pallas_call(
        functools.partial(prepare_kernel, dims),
        out_shape=(
            array(halves_z, ns, cx, cy, LANES),
            *(array(ns, TILE, nz),) * 4,
            array(*velocity.shape),
            array(1, ns),
            array(nr_rows, LANES, dtype=bf16),
            array(2 * ns8, 2 * nr_lanes, dtype=bf16),
            array(ns8, LANES),
            array(1, cells * halves_z, dtype=jnp.int32),
        ),
        in_specs=[vmem, vmem] + [hbm] * 7,
        out_specs=(vmem,) * 11,
        scratch_shapes=[
            pltpu.VMEM((LANES, nr_lanes), f32),
            pltpu.VMEM((ns, nr), jnp.int32),
            pltpu.VMEM((ns, nr), jnp.int32),
            pltpu.VMEM((1, ns), f32),
            pltpu.VMEM(codes.shape, f32),
            pltpu.SemaphoreType.DMA((cx, halves_z)),
            pltpu.SemaphoreType.DMA((6,)),
        ],
        compiler_params=pltpu.CompilerParams(vmem_limit_bytes=12 << 20),
        name="prepare",
    )(
        log_rates[None, :],
        substeps.reshape(1, cells * halves_z),
        *(
            pltpu.with_memory_space_constraint(value, pltpu.HBM)
            for value in (
                species,
                velocity,
                diffusivity[None, :],
                reactants.T,
                products.T,
                heat_weights[None, :],
                jnp.asarray(codes),
            )
        ),
    )
    sent = (row_a, row_b, col_a, col_b)

    def swap(value, axis, parity):
        pairs = []
        for low in range(parity, lax.axis_size(axis) - 1, 2):
            pairs += [(low, low + 1), (low + 1, low)]
        return lax.ppermute(value, axis, pairs)

    col_got = [swap(sent[2 + parity], "col", parity) for parity in range(2)]
    row_got = [swap(sent[parity], "row", parity) for parity in range(2)]
    got = (*row_got, *col_got)

    mv_all, heat = pl.pallas_call(
        functools.partial(inner_kernel, dims, inner_total, inner_group),
        out_shape=(array(*mv_shape), array(halves_z, cells, LANES)),
        in_specs=[smem, smem] + [vmem] * 5,
        out_specs=(vmem,) * 2,
        scratch_shapes=[
            pltpu.VMEM((ns8, inner_group * LANES), f32),
            pltpu.SMEM((MAXSUB + 2,), f32),
        ],
        compiler_params=pltpu.CompilerParams(vmem_limit_bytes=20 << 20),
        cost_estimate=estimate,
        name="inner",
    )(order, spread, sp, speed, rp, st, weight)
    table_z = jnp.asarray(cosine_table(nz))
    reacted, forward, _, *table_parts = pl.pallas_call(
        functools.partial(
            outer_kernel, dims, inner_total, outer_total, outer_group, rows_count, cols_count
        ),
        out_shape=(
            array(*species.shape),
            array(nz, LANES),
            array(*mv_shape),
            array(nz, nz, dtype=bf16),
            array(nz, nz, dtype=bf16),
        ),
        in_specs=[smem] * 2 + [vmem] * 8 + [anywhere] * 8,
        out_specs=(anywhere, vmem, vmem, vmem, vmem),
        scratch_shapes=[
            pltpu.VMEM((4, halves_z, ns, TILE, LANES), f32),
            pltpu.VMEM((ns8, outer_group * LANES), f32),
            pltpu.VMEM((halves_z, cells, LANES), f32),
            pltpu.SMEM((MAXSUB + 2,), f32),
            pltpu.SemaphoreType.DMA((4, halves_z)),
            pltpu.SemaphoreType.DMA((cx, halves_z)),
        ],
        input_output_aliases={4: 2},
        compiler_params=pltpu.CompilerParams(vmem_limit_bytes=20 << 20),
        cost_estimate=estimate,
        name="outer",
    )(
        order,
        spread,
        speed,
        divergence.reshape(cells, nz),
        mv_all,
        heat,
        rp,
        st,
        weight,
        table_z,
        *sent,
        *got,
    )
    pressure = solve(forward, table_parts, (rows_count, cols_count, depth, cx, cy))
    return reacted, pressure.reshape(cx, cy, nz)


def solve(forward, table_parts, dims):
    rows_count, cols_count, depth, cx, cy = dims
    device_count = rows_count * cols_count
    nz = device_count * depth
    na, nb = rows_count * cx, cols_count * cy
    nb_pad = round_up(nb, LANES)
    aligned = depth % TILE == 0

    def exchange(value):
        value = value.reshape(device_count, depth, LANES)
        value = lax.all_to_all(value, ("row", "col"), split_axis=0, concat_axis=0, tiled=True)
        return value

    table_y = np.zeros((nb, nb_pad), np.float32)
    table_y[:, :nb] = cosine_table(nb).T
    table_x = cosine_table(na).reshape(na, rows_count, cx)
    mix_x = np.einsum("arx,kl->kaxrl", table_x, np.eye(depth, dtype=np.float32))
    mix_x = mix_x.reshape(depth * na, cx * rows_count * depth)
    base = np.full((na, nb_pad), 1.0, np.float64)
    base[:, :nb] = screen + mode_values(na)[:, None] + mode_values(nb)[None, :]
    planes = exchange(forward)
    group = rows_count * depth
    if aligned:
        planes = planes.reshape(nz, LANES)
        shape = (nz, LANES)
    else:
        planes = planes.reshape(rows_count, cols_count, depth, LANES).transpose(1, 0, 2, 3)
        shape = (cols_count, group, LANES)
        planes = planes.reshape(shape)
    outgoing = pl.pallas_call(
        functools.partial(solve_kernel, dims),
        out_shape=jax.ShapeDtypeStruct(shape, f32),
        in_specs=[smem, vmem, vmem, vmem, vmem],
        out_specs=vmem,
        scratch_shapes=[
            pltpu.VMEM((cols_count, cx * cy, cx * nb_pad), f32),
            pltpu.VMEM((cx * group, nb_pad), f32),
        ],
        compiler_params=pltpu.CompilerParams(vmem_limit_bytes=40 << 20),
        name="solve",
    )(
        jnp.asarray(mode_values(nz).astype(np.float32)),
        planes,
        jnp.asarray(table_y),
        jnp.asarray(mix_x),
        jnp.asarray(base.astype(np.float32)),
    )
    if not aligned:
        outgoing = outgoing.reshape(cols_count, rows_count, depth, LANES).transpose(1, 0, 2, 3)
    columns = exchange(outgoing).reshape(nz, LANES)
    return pl.pallas_call(
        inverse_kernel,
        out_shape=jax.ShapeDtypeStruct((cx * cy, nz), f32),
        in_specs=[vmem] * 3,
        out_specs=vmem,
        name="inverse",
    )(columns, *table_parts)


def solution(mesh):
    return jax.shard_map(
        local,
        mesh=mesh,
        in_specs=(
            P(None, "row", "col", None),
            P(None, "row", "col", None),
            P(),
            P("row", "col", None),
            P(),
            P(),
            P(),
            P(),
            P("row", "col", None),
        ),
        out_specs=(P(None, "row", "col", None), P("row", "col", None)),
        check_vma=False,
    )
```

profile of v0, /device:TPU:0, one launch (start us, length us, event | category | flops | bytes accessed | tf_op | source)
XLA Modules:
  0.0 96.0 jit_solution(4517699424650697554)
XLA Ops:
  0.6 0.7 broadcast_in_dim.9.log_rates
  1.3 0.8 copy.19
  2.1 0.1 reshape.25.substeps
  2.3 2.8 %prepare.1 = (f32[2,53,8,8,128]{4,3,2,1,0:T(8,128)S(1)}, f32[53,8,256]{2,1,0:T(8,128)S(1)}, f32[53,8,256]{2,1,0:T(8,128)S(1)}, f32[53,8,256]{2,1,0:T(8,128)S(1)}...) custom-call(f32[1,325]{1,0:T(1,128)S(1)} %broadcast_in_dim.9.log_rat, ...), custom_call_target="tpu_custom_call" | custom-call | tf_op jit(solution)/shard_map/prepare/pallas_call | solution.py:610
  5.1 3.1 %collective-permute-start = (f32[53,8,256]{2,1,0:T(8,128)S(1)}, f32[53,8,256]{2,1,0:T(8,128)S(1)}, u32[]{:S(2)}, u32[]{:S(2)}) collective-permute-start(f32[53,8,256]{2,1,0:T(8,128)S(1)} %get-tuple-element.28.row_sent_a), channel_id=1, source_target_pairs={{0,8},{8,0},{16,24},{24,16},{1,9},{9,1},{17,25},{25,17},{2,10},{10... | collective-permute-start | bytes 1302536 | tf_op jit(solution)/shard_map/ppermute | solution.py:657
  8.2 0.7 collective-permute-start.1
  8.9 0.1 collective-permute-start.2
  8.9 0.7 collective-permute-start.3
  9.6 0.0 copy-start.6
  9.7 0.0 copy-start.7
  9.7 37.2 %inner.1 = (f32[10,2,448,128]{3,2,1,0:T(8,128)S(1)}, f32[2,64,128]{2,1,0:T(8,128)S(1)}) custom-call(s32[1,128]{1,0:T(1,128)S(1)} %get-tuple-element.19.order, f32[1,53]{1,0:T(1,128)S(1)} %get-tuple-element.20.diffusivity, f32[2,53,8,8,128]{4,3,2,1,0:T(8,128)S(1)} %get-tuple-element.22.sp, f32[3,8,8,256]{3,2,1,0:T(8,128)S(1)} %get-tuple-element.21.velocity, ...), custom_call_target="tpu_custom_call" | custom-call | flops 10000000000 | bytes 10000000 | tf_op jit(solution)/shard_map/inner/pallas_call | solution.py:663
  46.9 0.0 collective-permute-done.row_got_a
  46.9 0.0 collective-permute-done.1.row_got_b
  46.9 0.0 collective-permute-done.2.col_got_a
  46.9 0.0 collective-permute-done.3.col_got_b
  47.0 0.0 copy-start
  47.0 0.0 copy-start.3
  47.0 0.0 copy-start.4
  47.0 0.0 copy-start.5
  47.0 19.3 %outer.1 = (f32[53,8,8,256]{3,2,1,0:T(8,128)}, f32[256,128]{1,0:T(8,128)S(1)}, f32[10,2,448,128]{3,2,1,0:T(8,128)S(1)}, bf16[256,256]{1,0:T(8,128)(2,1)S(1)}, bf16[256,256]{1,0:T(8,128)(2,1)S(1)}) custom-call(s32[1,128]{1,0:T(1,128)S(1)} %get-tuple-element.19.order, f32[1,53]{1,0:T(1,128)S(1)} %get-tuple-element.20.diffusivity, ...), custom_call_target="tpu_custom_call", output_to_operand_aliasing={{2}: (4, {})} | custom-call | flops 10000000000 | bytes 10000000 | tf_op jit(solution)/shard_map/outer/pallas_call | solution.py:677
  66.4 14.7 %all_to_all.10 = f32[32,8,128]{2,1,0:T(8,128)S(1)} all-to-all(f32[32,8,128]{2,1,0:T(8,128)S(1)} %bitcast.12), channel_id=1, replica_groups=mesh['row'=4,'col'=8] {'row','col'}, dimensions={0} | all-to-all | bytes 262144 | tf_op jit(solution)/shard_map/all_to_all | solution.py:730
  81.1 2.4 %solve.1 = f32[256,128]{1,0:T(8,128)S(1)} custom-call(f32[256]{0:T(256)S(1)} %copy-done.5, f32[256,128]{1,0:T(8,128)S(1)} %bitcast.10, f32[64,128]{1,0:T(8,128)S(1)} %copy-done.3, f32[256,256]{1,0:T(8,128)S(1)} %copy-done, f32[32,128]{1,0:T(8,128)S(1)} %copy-done.4), custom_call_target="tpu_custom_call" | custom-call | tf_op jit(solution)/shard_map/solve/pallas_call | solution.py:749
  83.5 10.6 %all_to_all.11 = f32[32,8,128]{2,1,0:T(8,128)} all-to-all(f32[32,8,128]{2,1,0:T(8,128)S(1)} %bitcast.11), channel_id=1, replica_groups=mesh['row'=4,'col'=8] {'row','col'}, dimensions={0} | all-to-all | bytes 262144 | tf_op jit(solution)/shard_map/all_to_all | solution.py:730
  94.1 1.9 %inverse.1 = f32[64,256]{1,0:T(8,128)} custom-call(f32[256,128]{1,0:T(8,128)} %bitcast.14, bf16[256,256]{1,0:T(8,128)(2,1)} %copy-done.1, bf16[256,256]{1,0:T(8,128)(2,1)} %copy-done.2), custom_call_target="tpu_custom_call" | custom-call | tf_op jit(solution)/shard_map/inverse/pallas_call | solution.py:770
  (10 shorter events, 0.0 us)
Async XLA Ops:
  5.1 41.8 %collective-permute-start = (f32[53,8,256]{2,1,0:T(8,128)S(1)}, f32[53,8,256]{2,1,0:T(8,128)S(1)}, u32[]{:S(2)}, u32[]{:S(2)}) collective-permute-start(f32[53,8,256]{2,1,0:T(8,128)S(1)} %get-tuple-element.28.row_sent_a), channel_id=1, source_target_pairs={{0,8},{8,0},{16,24},{24,16},{1,9},{9,1},{17,25},{25,17},{2,10},{10... | collective-permute-start | bytes 1302536 | tf_op jit(solution)/shard_map/ppermute | solution.py:657
  8.2 38.7 %collective-permute-start.1 = (f32[53,8,256]{2,1,0:T(8,128)S(1)}, f32[53,8,256]{2,1,0:T(8,128)S(1)}, u32[]{:S(2)}, u32[]{:S(2)}) collective-permute-start(f32[53,8,256]{2,1,0:T(8,128)S(1)} %get-tuple-element.29.row_sent_b), channel_id=1, source_target_pairs={{8,16},{16,8},{9,17},{17,9},{10,18},{18,10},{11,19},{19,11},{12,20... | collective-permute-start | bytes 1302536 | tf_op jit(solution)/shard_map/ppermute | solution.py:657
  8.9 38.1 %collective-permute-start.2 = (f32[53,8,256]{2,1,0:T(8,128)S(1)}, f32[53,8,256]{2,1,0:T(8,128)S(1)}, u32[]{:S(2)}, u32[]{:S(2)}) collective-permute-start(f32[53,8,256]{2,1,0:T(8,128)S(1)} %get-tuple-element.30.col_sent_a), channel_id=1, source_target_pairs={{0,1},{1,0},{2,3},{3,2},{4,5},{5,4},{6,7},{7,6},{8,9},{9,8},{10,11... | collective-permute-start | bytes 1302536 | tf_op jit(solution)/shard_map/ppermute | solution.py:657
  8.9 38.0 %collective-permute-start.3 = (f32[53,8,256]{2,1,0:T(8,128)S(1)}, f32[53,8,256]{2,1,0:T(8,128)S(1)}, u32[]{:S(2)}, u32[]{:S(2)}) collective-permute-start(f32[53,8,256]{2,1,0:T(8,128)S(1)} %get-tuple-element.31.col_sent_b), channel_id=1, source_target_pairs={{1,2},{2,1},{3,4},{4,3},{5,6},{6,5},{9,10},{10,9},{11,12},{12,11},... | collective-permute-start | bytes 1302536 | tf_op jit(solution)/shard_map/ppermute | solution.py:657
  9.6 37.3 %copy-start.6 = (f32[8,8,256]{2,1,0:T(8,128)S(1)}, f32[8,8,256]{2,1,0:T(8,128)}, u32[]{:S(2)}) copy-start(f32[8,8,256]{2,1,0:T(8,128)} %param.18) | copy-start | bytes 196612
  9.7 37.3 %copy-start.7 = (f32[256,256]{1,0:T(8,128)S(1)}, f32[256,256]{1,0:T(8,128)}, u32[]{:S(2)}) copy-start(f32[256,256]{1,0:T(8,128)} %constant.13.clone.table_z) | copy-start | bytes 786436
  47.0 34.1 %copy-start = (f32[256,256]{1,0:T(8,128)S(1)}, f32[256,256]{1,0:T(8,128)}, u32[]{:S(2)}) copy-start(f32[256,256]{1,0:T(8,128)} %constant.16.clone.mix_x) | copy-start | bytes 786436
  47.0 34.1 %copy-start.3 = (f32[64,128]{1,0:T(8,128)S(1)}, f32[64,128]{1,0:T(8,128)}, u32[]{:S(2)}) copy-start(f32[64,128]{1,0:T(8,128)} %constant.15.clone.table_y) | copy-start | bytes 98308
  47.0 34.1 %copy-start.4 = (f32[32,128]{1,0:T(8,128)S(1)}, f32[32,128]{1,0:T(8,128)}, u32[]{:S(2)}) copy-start(f32[32,128]{1,0:T(8,128)} %constant.17.clone.base) | copy-start | bytes 49156
  47.0 34.1 %copy-start.5 = (f32[256]{0:T(256)S(1)}, f32[256]{0:T(256)}, u32[]{:S(2)}) copy-start(f32[256]{0:T(256)} %constant.14.clone.lam_z) | copy-start | bytes 3076
  66.4 14.7 %copy-start.1 = (bf16[256,256]{1,0:T(8,128)(2,1)}, bf16[256,256]{1,0:T(8,128)(2,1)S(1)}, u32[]{:S(2)}) copy-start(bf16[256,256]{1,0:T(8,128)(2,1)S(1)} %get-tuple-element.34.table_high) | copy-start | bytes 393220
  66.4 14.7 %copy-start.2 = (bf16[256,256]{1,0:T(8,128)(2,1)}, bf16[256,256]{1,0:T(8,128)(2,1)S(1)}, u32[]{:S(2)}) copy-start(bf16[256,256]{1,0:T(8,128)(2,1)S(1)} %get-tuple-element.35.table_low) | copy-start | bytes 393220
where the time goes:
time: 94.7 us; the launch traced here: 96 us
  Pallas kernels  63.7 us (67%)
  blocking collectives  25.3 us (27%)
  starting transfers between devices  4.55 us (5%)
  local copies, waits for them, and re-layouts  1.68 us (2%)
    pallas_call x1, Pallas kernels, local(): pl.pallas_call(functools.partial(inner_kernel, dims, inner_total, inner_g...  37.2 us
    all_to_all x2, blocking collectives, exchange(): lax.all_to_all(value, ('row', 'col'), split_axis=0, concat_axis=0, tiled=...  25.3 us
    pallas_call x1, Pallas kernels, local(): pl.pallas_call(functools.partial(outer_kernel, dims, inner_total, outer_t...  19.3 us
    ppermute x4, starting transfers between devices, swap(): return lax.ppermute(value, axis, pairs)  4.55 us
    pallas_call x1, Pallas kernels, local(): pl.pallas_call(functools.partial(prepare_kernel, dims), out_shape=(array(...  2.79 us
    pallas_call x1, Pallas kernels, solve(): pl.pallas_call(functools.partial(solve_kernel, dims), out_shape=jax.Shape...  2.4 us
    pallas_call x1, Pallas kernels, solve(): pl.pallas_call(inverse_kernel, out_shape=jax.ShapeDtypeStruct((cx * cy, n...  1.9 us
  transfers between devices with their start and end apart: 4, of which 0 were waited for; matrix products, arithmetic and copies ran while one was open for 0% of the time, Pallas kernels for 39%

commit v1 on v0

--- a/solution.py
+++ b/solution.py
@@ -143,7 +143,7 @@
     lax.fori_loop(0, total // group, one_group, 0)
 
 
-def over_species(ns, body, unroll=4):
+def over_species(ns, body, unroll=18):
     def step(i, carry):
         for j in range(unroll):
             body(i * unroll + j)
@@ -156,8 +156,6 @@
 
 def prepare_kernel(
     dims,
-    log_rates,
-    substeps,
     species_hbm,
     velocity_hbm,
     diffusivity_hbm,
@@ -165,6 +163,8 @@
     products_hbm,
     weights_hbm,
     codes_hbm,
+    rates_hbm,
+    substeps_hbm,
     sp,
     row_a,
     row_b,
@@ -181,6 +181,9 @@
     products,
     heat_weights,
     codes,
+    log_rates,
+    substeps,
+    counts,
     in_sem,
     small_sem,
 ):
@@ -202,19 +205,31 @@
                 (weights_hbm, heat_weights),
                 (codes_hbm, codes),
                 (diffusivity_hbm, diffusivity),
+                (rates_hbm, log_rates),
+                (substeps_hbm, substeps),
                 (velocity_hbm, velocity),
             )
         )
     ]
-    for copy in small[:5]:
+    for copy in small[:-1]:
         copy.start()
     for x in range(cx):
         for z in range(halves_z):
             load(x, z).start()
-    small[5].start()
-    for copy in small[:5]:
+    small[-1].start()
+    for copy in small[:-1]:
         copy.wait()
-    order_row[...] = sort_blocks(substeps[...].astype(f32), codes[0:1, :], codes[1:2, :])
+    blocks = order_row.shape[1]
+    counts[...] = jnp.zeros_like(counts)
+    for x in range(cx):
+        counts[x * halves_z : (x + 1) * halves_z, 0:cy] = substeps[x].astype(f32)
+    down = lax.broadcasted_iota(jnp.int32, (LANES, blocks), 0)
+    across = lax.broadcasted_iota(jnp.int32, (LANES, blocks), 1)
+    repeat = jnp.where(lax.rem(across, cy) == down, 1.0, 0.0).astype(bf16)
+    repeated = jnp.dot(counts[...].astype(bf16), repeat, preferred_element_type=f32)
+    mine = lax.div(across, cy)[: counts.shape[0]] == down[: counts.shape[0]]
+    flat_counts = jnp.sum(jnp.where(mine, repeated, 0.0), axis=0, keepdims=True)
+    order_row[...] = sort_blocks(flat_counts, codes[0:1, :], codes[1:2, :])
     react = reactants[...].astype(f32)
     build[...] = jnp.zeros_like(build)
     build[0:ns, 0:nr] = react
@@ -252,7 +267,7 @@
             col_b[s, :, q] = flat[z, pl.ds(s * cx * cy + cy - 1 - y_a, cx, stride=cy), :]
 
     over_species(ns, body)
-    small[5].wait()
+    small[-1].wait()
 
 
 def fill_steps(steps):
@@ -387,7 +402,6 @@
     row_got_b,
     col_got_a,
     col_got_b,
-    reacted_hbm,
     forward,
     mv,
     table_high,
@@ -397,7 +411,6 @@
     heat,
     steps,
     halo_sem,
-    out_sem,
 ):
     ns, cx, cy, halves_z = dims
     fill_steps(steps)
@@ -474,32 +487,38 @@
     refs = (order, steps, mv, conc, rp_ref, st_ref, heat, weight_ref)
     react_blocks(first_block, total, group, refs, target_of)
 
-    def save(x, z):
-        plane = {0: base, cx - 1: base + 1}.get(x, x - 1)
-        tiles = mv.reshape(cx + 2, halves_z, conc.shape[0], TILE, LANES)
-        return pltpu.make_async_copy(
-            tiles.at[plane, z, 0:ns], reacted_hbm.at[:, x, :, lanes[z]], out_sem.at[x, z]
-        )
-
-    for x in range(cx):
-        for z in range(halves_z):
-            save(x, z).start()
     heat_all = jnp.concatenate([heat[z] for z in range(halves_z)], axis=1)
     source = divergence[...] - heat_all / time_step
     table_high[...], table_low[...] = halves(table_z[...])
     result = dot_halves((table_high[...], table_low[...]), halves(source), ((1,), (1,)))
-    forward[...] = jnp.zeros_like(forward)
-    forward[:, 0 : cx * cy] = result
+    rows = forward.shape[0]
+    sections = [result[i * rows : (i + 1) * rows] for i in range(LANES // (cx * cy))]
+    forward[...] = jnp.concatenate(sections, axis=1)
+
+
+def solve_kernel(
+    dims, lam_z, planes, table_y, mix_x, base, mv, out, reacted_hbm, wide, tall, out_sem
+):
+    rows_count, cols_count, depth, cx, cy = dims
+    ns, halves_z = reacted_hbm.shape[0], mv.shape[1]
+    tiles = mv.reshape(*mv.shape[:2], mv.shape[2] // TILE, TILE, LANES)
+
+    def save(x, z):
+        plane = {0: cx - 2, cx - 1: cx - 1}.get(x, x - 1)
+        return pltpu.make_async_copy(
+            tiles.at[plane, z, 0:ns],
+            reacted_hbm.at[:, x, :, pl.ds(z * LANES, LANES)],
+            out_sem.at[x, z],
+        )
+
     for x in range(cx):
         for z in range(halves_z):
-            save(x, z).wait()
-
-
-def solve_kernel(dims, lam_z, planes, table_y, mix_x, base, out, wide, tall):
-    rows_count, cols_count, depth, cx, cy = dims
+            save(x, z).start()
     cells = cx * cy
     nb = base.shape[1]
     na = rows_count * cx
+    sections = LANES // cells
+    run = depth // sections
     device = lax.axis_index("row") * cols_count + lax.axis_index("col")
     group = rows_count * depth
     total = jnp.zeros((group, cx * nb), f32)
@@ -507,17 +526,12 @@
         wide[c] = jnp.zeros((cells, cx * nb), f32)
         for x in range(cx):
             wide[c, x * cy : (x + 1) * cy, x * nb : (x + 1) * nb] = table_y[c * cy : (c + 1) * cy, :]
-        if planes.ndim == 2:
-            block = jnp.concatenate(
-                [
-                    planes[(r * cols_count + c) * depth : (r * cols_count + c + 1) * depth, 0:cells]
-                    for r in range(rows_count)
-                ],
-                axis=0,
-            )
-        else:
-            block = planes[c, :, 0:cells]
-        total = total + dot3(block, wide[c])
+        starts = [(r * cols_count + c) * run for r in range(rows_count)]
+        block = jnp.concatenate([planes[at : at + run, :] for at in starts], axis=0)
+        block = jnp.concatenate(
+            [pltpu.roll(block, (LANES - i * cells) % LANES, 1) for i in range(sections)], axis=0
+        )
+        total = total + dot3(block[:, 0:cells], wide[c])
     for x in range(cx):
         tall[x * group : (x + 1) * group, :] = total[:, x * nb : (x + 1) * nb]
     spectrum = dot3(mix_x[...], tall[...])
@@ -528,20 +542,24 @@
     spectrum = jnp.concatenate(solved, axis=0)
     back = dot3(mix_x[...], spectrum, ((0,), (0,)))
     row = jnp.concatenate([back[x * group : (x + 1) * group] for x in range(cx)], axis=1)
-    out[...] = jnp.zeros_like(out)
     for c in range(cols_count):
         block = dot3(row, wide[c], ((1,), (1,)))
-        if planes.ndim == 2:
+        for i in range(sections):
             for r in range(rows_count):
-                at = (r * cols_count + c) * depth
-                out[at : at + depth, 0:cells] = block[r * depth : (r + 1) * depth]
-        else:
-            out[c, :, 0:cells] = block
+                at = (r * cols_count + c) * run
+                start = (i * rows_count + r) * run
+                out[at : at + run, i * cells : (i + 1) * cells] = block[start : start + run]
+    for x in range(cx):
+        for z in range(halves_z):
+            save(x, z).wait()
 
 
 def inverse_kernel(columns, table_high, table_low, out):
     cells = out.shape[0]
-    out[...] = dot_halves(halves(columns[...].T[:cells]), (table_high[...], table_low[...]))
+    turned = columns[...].T
+    sections = [turned[i * cells : (i + 1) * cells] for i in range(LANES // cells)]
+    turned = jnp.concatenate(sections, axis=1)
+    out[...] = dot_halves(halves(turned), (table_high[...], table_low[...]))
 
 
 smem = pl.BlockSpec(memory_space=pltpu.SMEM)
@@ -594,9 +612,9 @@
             else:
                 slot, at = cx + (y > 0), x
             for z in range(halves_z):
-                flat = (x * cy + y) * halves_z + z
-                codes[0, flat] = flat << 8 | slot << 4 | at << 1 | z
-                codes[1, flat] = 8.0 * inside
+                block = (x * halves_z + z) * cy + y
+                codes[0, block] = (x * cy + y) << 9 | slot << 4 | at << 1 | z
+                codes[1, block] = 8.0 * inside
                 inner_total += inside
     outer_total = cells * halves_z - inner_total
     inner_group = pick_group(inner_total, 12)
@@ -619,7 +637,7 @@
             array(ns8, LANES),
             array(1, cells * halves_z, dtype=jnp.int32),
         ),
-        in_specs=[vmem, vmem] + [hbm] * 7,
+        in_specs=[hbm] * 9,
         out_specs=(vmem,) * 11,
         scratch_shapes=[
             pltpu.VMEM((LANES, nr_lanes), f32),
@@ -627,14 +645,15 @@
             pltpu.VMEM((ns, nr), jnp.int32),
             pltpu.VMEM((1, ns), f32),
             pltpu.VMEM(codes.shape, f32),
+            pltpu.VMEM((1, nr), f32),
+            pltpu.VMEM((cx, halves_z, cy), jnp.int32),
+            pltpu.VMEM((cx * halves_z, LANES), f32),
             pltpu.SemaphoreType.DMA((cx, halves_z)),
-            pltpu.SemaphoreType.DMA((6,)),
+            pltpu.SemaphoreType.DMA((8,)),
         ],
         compiler_params=pltpu.CompilerParams(vmem_limit_bytes=12 << 20),
         name="prepare",
     )(
-        log_rates[None, :],
-        substeps.reshape(1, cells * halves_z),
         *(
             pltpu.with_memory_space_constraint(value, pltpu.HBM)
             for value in (
@@ -645,6 +664,8 @@
                 products.T,
                 heat_weights[None, :],
                 jnp.asarray(codes),
+                log_rates[None, :],
+                substeps.transpose(0, 2, 1),
             )
         ),
     )
@@ -673,29 +694,30 @@
         cost_estimate=estimate,
         name="inner",
     )(order, spread, sp, speed, rp, st, weight)
-    table_z = jnp.asarray(cosine_table(nz))
-    reacted, forward, _, *table_parts = pl.pallas_call(
+    sections = LANES // cells
+    order_z = np.arange(nz).reshape(device_count, sections, depth // sections)
+    order_z = order_z.transpose(1, 0, 2).reshape(nz)
+    table_z = jnp.asarray(cosine_table(nz)[order_z])
+    forward, mv_all, *table_parts = pl.pallas_call(
         functools.partial(
             outer_kernel, dims, inner_total, outer_total, outer_group, rows_count, cols_count
         ),
         out_shape=(
-            array(*species.shape),
-            array(nz, LANES),
+            array(nz // sections, LANES),
             array(*mv_shape),
             array(nz, nz, dtype=bf16),
             array(nz, nz, dtype=bf16),
         ),
         in_specs=[smem] * 2 + [vmem] * 8 + [anywhere] * 8,
-        out_specs=(anywhere, vmem, vmem, vmem, vmem),
+        out_specs=(vmem,) * 4,
         scratch_shapes=[
             pltpu.VMEM((4, halves_z, ns, TILE, LANES), f32),
             pltpu.VMEM((ns8, outer_group * LANES), f32),
             pltpu.VMEM((halves_z, cells, LANES), f32),
             pltpu.SMEM((MAXSUB + 2,), f32),
             pltpu.SemaphoreType.DMA((4, halves_z)),
-            pltpu.SemaphoreType.DMA((cx, halves_z)),
         ],
-        input_output_aliases={4: 2},
+        input_output_aliases={4: 1},
         compiler_params=pltpu.CompilerParams(vmem_limit_bytes=20 << 20),
         cost_estimate=estimate,
         name="outer",
@@ -713,49 +735,46 @@
         *sent,
         *got,
     )
-    pressure = solve(forward, table_parts, (rows_count, cols_count, depth, cx, cy))
+    dims = (rows_count, cols_count, depth, cx, cy)
+    reacted, pressure = solve(forward, table_parts, mv_all, array(*species.shape), dims)
     return reacted, pressure.reshape(cx, cy, nz)
 
 
-def solve(forward, table_parts, dims):
+def solve(forward, table_parts, mv, reacted_shape, dims):
     rows_count, cols_count, depth, cx, cy = dims
     device_count = rows_count * cols_count
     nz = device_count * depth
     na, nb = rows_count * cx, cols_count * cy
     nb_pad = round_up(nb, LANES)
-    aligned = depth % TILE == 0
+    sections = LANES // (cx * cy)
+    run = depth // sections
+    group = rows_count * depth
 
     def exchange(value):
-        value = value.reshape(device_count, depth, LANES)
+        value = value.reshape(device_count, run, LANES)
         value = lax.all_to_all(value, ("row", "col"), split_axis=0, concat_axis=0, tiled=True)
-        return value
+        return value.reshape(device_count * run, LANES)
 
     table_y = np.zeros((nb, nb_pad), np.float32)
     table_y[:, :nb] = cosine_table(nb).T
     table_x = cosine_table(na).reshape(na, rows_count, cx)
-    mix_x = np.einsum("arx,kl->kaxrl", table_x, np.eye(depth, dtype=np.float32))
-    mix_x = mix_x.reshape(depth * na, cx * rows_count * depth)
+    same = np.eye(depth, dtype=np.float32).reshape(depth, sections, run)
+    mix_x = np.einsum("arx,kij->kaxirj", table_x, same)
+    mix_x = mix_x.reshape(depth * na, cx * group)
     base = np.full((na, nb_pad), 1.0, np.float64)
     base[:, :nb] = screen + mode_values(na)[:, None] + mode_values(nb)[None, :]
     planes = exchange(forward)
-    group = rows_count * depth
-    if aligned:
-        planes = planes.reshape(nz, LANES)
-        shape = (nz, LANES)
-    else:
-        planes = planes.reshape(rows_count, cols_count, depth, LANES).transpose(1, 0, 2, 3)
-        shape = (cols_count, group, LANES)
-        planes = planes.reshape(shape)
-    outgoing = pl.pallas_call(
+    outgoing, reacted = pl.pallas_call(
         functools.partial(solve_kernel, dims),
-        out_shape=jax.ShapeDtypeStruct(shape, f32),
-        in_specs=[smem, vmem, vmem, vmem, vmem],
-        out_specs=vmem,
+        out_shape=(jax.ShapeDtypeStruct(planes.shape, f32), reacted_shape),
+        in_specs=[smem, vmem, vmem, vmem, vmem, vmem],
+        out_specs=(vmem, anywhere),
         scratch_shapes=[
             pltpu.VMEM((cols_count, cx * cy, cx * nb_pad), f32),
             pltpu.VMEM((cx * group, nb_pad), f32),
+            pltpu.SemaphoreType.DMA((cx, mv.shape[1])),
         ],
-        compiler_params=pltpu.CompilerParams(vmem_limit_bytes=40 << 20),
+        compiler_params=pltpu.CompilerParams(vmem_limit_bytes=16 << 20),
         name="solve",
     )(
         jnp.asarray(mode_values(nz).astype(np.float32)),
@@ -763,17 +782,18 @@
         jnp.asarray(table_y),
         jnp.asarray(mix_x),
         jnp.asarray(base.astype(np.float32)),
+        mv,
     )
-    if not aligned:
-        outgoing = outgoing.reshape(cols_count, rows_count, depth, LANES).transpose(1, 0, 2, 3)
-    columns = exchange(outgoing).reshape(nz, LANES)
-    return pl.pallas_call(
+    columns = exchange(outgoing)
+    pressure = pl.pallas_call(
         inverse_kernel,
         out_shape=jax.ShapeDtypeStruct((cx * cy, nz), f32),
         in_specs=[vmem] * 3,
         out_specs=vmem,
+        compiler_params=pltpu.CompilerParams(vmem_limit_bytes=4 << 20),
         name="inverse",
     )(columns, *table_parts)
+    return reacted, pressure
 
 
 def solution(mesh):

time: 94.7 us -> 85.8 us (0.906); the launches traced: 96 us -> 86.1 us
  Pallas kernels: 63.7 us -> 35.1 us
  blocking collectives: 25.3 us -> 44.3 us
    pallas_call x1, Pallas kernels: 37.2 us -> 13.6 us  [local(): pl.pallas_call(functools.partial(inner_kernel, dims, inner_total, inner_g...]
    all_to_all x2, blocking collectives: 25.3 us -> 44.3 us  [exchange(): lax.all_to_all(value, ('row', 'col'), split_axis=0, concat_axis=0, tiled=...]
    pallas_call x1, Pallas kernels: 19.3 us -> 14.6 us  [local(): pl.pallas_call(functools.partial(outer_kernel, dims, inner_total, outer_t...]
    pallas_call x1, Pallas kernels: 1.9 us -> 0.89 us  [solve(): pl.pallas_call(inverse_kernel, out_shape=jax.ShapeDtypeStruct((cx * cy, n...]
  transfers between devices with their start and end apart: 4 -> 4, of which waited for: 0 -> 0; matrix products, arithmetic and copies ran while one was open for 0% -> 0% of each run, Pallas kernels for 39% -> 16%
where the time goes in v1:
time: 85.8 us; the launch traced here: 86.1 us
  blocking collectives  44.3 us (52%)
  Pallas kernels  35.1 us (41%)
  starting transfers between devices  4.55 us (5%)
  local copies, waits for them, and re-layouts  1.29 us (2%)
    all_to_all x2, blocking collectives, exchange(): lax.all_to_all(value, ('row', 'col'), split_axis=0, concat_axis=0, tiled=...  44.3 us
    pallas_call x1, Pallas kernels, local(): pl.pallas_call(functools.partial(outer_kernel, dims, inner_total, outer_t...  14.6 us
    pallas_call x1, Pallas kernels, local(): pl.pallas_call(functools.partial(inner_kernel, dims, inner_total, inner_g...  13.6 us
    ppermute x4, starting transfers between devices, swap(): return lax.ppermute(value, axis, pairs)  4.55 us
    pallas_call x1, Pallas kernels, solve(): pl.pallas_call(functools.partial(solve_kernel, dims), out_shape=(jax.Shap...  3.29 us
    pallas_call x1, Pallas kernels, local(): pl.pallas_call(functools.partial(prepare_kernel, dims), out_shape=(array(...  2.81 us
  transfers between devices with their start and end apart: 4, of which 0 were waited for; matrix products, arithmetic and copies ran while one was open for 0% of the time, Pallas kernels for 16%

profile of v1, /device:TPU:0, one launch (start us, length us, event | category | flops | bytes accessed | tf_op | source)
XLA Modules:
  0.0 86.1 jit_solution(16855915101506534291)
XLA Ops:
  0.6 1.2 %broadcast_in_dim.11.rates_hbm = f32[1,325]{1,0:T(1,128)} reshape(f32[325]{0:T(512)} %param.19) | data formatting | bytes 2600 | tf_op jit(solution)/shard_map/broadcast_in_dim | solution.py:667
  1.9 2.8 %prepare.1 = (f32[2,53,8,8,128]{4,3,2,1,0:T(8,128)S(1)}, f32[53,8,256]{2,1,0:T(8,128)S(1)}, f32[53,8,256]{2,1,0:T(8,128)S(1)}, f32[53,8,256]{2,1,0:T(8,128)S(1)}...) custom-call(f32[53,8,8,256]{3,2,1,0:T(8,128)} %species_hbm.1, ...), custom_call_target="tpu_custom_call" | custom-call | tf_op jit(solution)/shard_map/prepare/pallas_call | solution.py:628
  4.7 3.1 %collective-permute-start = (f32[53,8,256]{2,1,0:T(8,128)S(1)}, f32[53,8,256]{2,1,0:T(8,128)S(1)}, u32[]{:S(2)}, u32[]{:S(2)}) collective-permute-start(f32[53,8,256]{2,1,0:T(8,128)S(1)} %get-tuple-element.30.row_sent_a), channel_id=1, source_target_pairs={{0,8},{8,0},{16,24},{24,16},{1,9},{9,1},{17,25},{25,17},{2,10},{10... | collective-permute-start | bytes 1302536 | tf_op jit(solution)/shard_map/ppermute | solution.py:678
  7.8 0.7 collective-permute-start.1
  8.5 0.1 collective-permute-start.2
  8.6 0.7 collective-permute-start.3
  9.3 0.0 copy-start.4
  9.3 0.0 copy-start.5
  9.3 13.6 %inner.1 = (f32[10,2,448,128]{3,2,1,0:T(8,128)S(1)}, f32[2,64,128]{2,1,0:T(8,128)S(1)}) custom-call(s32[1,128]{1,0:T(1,128)S(1)} %get-tuple-element.21.order, f32[1,53]{1,0:T(1,128)S(1)} %get-tuple-element.22.diffusivity, f32[2,53,8,8,128]{4,3,2,1,0:T(8,128)S(1)} %get-tuple-element.24.sp, f32[3,8,8,256]{3,2,1,0:T(8,128)S(1)} %get-tuple-element.23.velocity, ...), custom_call_target="tpu_custom_call" | custom-call | flops 10000000000 | bytes 10000000 | tf_op jit(solution)/shard_map/inner/pallas_call | solution.py:684
  22.9 0.0 collective-permute-done.row_got_a
  22.9 0.0 collective-permute-done.1.row_got_b
  22.9 0.0 collective-permute-done.2.col_got_a
  22.9 0.0 collective-permute-done.3.col_got_b
  22.9 0.0 copy-done.4
  22.9 0.0 copy-start
  22.9 0.0 copy-start.1
  22.9 0.0 copy-start.2
  23.0 0.0 copy-start.3
  23.0 14.6 %outer.1 = (f32[128,128]{1,0:T(8,128)S(1)}, f32[10,2,448,128]{3,2,1,0:T(8,128)S(1)}, bf16[256,256]{1,0:T(8,128)(2,1)S(1)}, bf16[256,256]{1,0:T(8,128)(2,1)S(1)}) custom-call(s32[1,128]{1,0:T(1,128)S(1)} %get-tuple-element.21.order, f32[1,53]{1,0:T(1,128)S(1)} %get-tuple-element.22.diffusivity, ...), custom_call_target="tpu_custom_call", output_to_operand_aliasing={{1}: (4, {})} | custom-call | flops 10000000000 | bytes 10000000 | tf_op jit(solution)/shard_map/outer/pallas_call | solution.py:701
  37.6 35.2 %all_to_all.10 = f32[32,4,128]{2,1,0:T(4,128)S(1)} all-to-all(f32[32,4,128]{2,1,0:T(4,128)S(1)} %bitcast.13), channel_id=1, replica_groups=mesh['row'=4,'col'=8] {'row','col'}, dimensions={0} | all-to-all | bytes 131072 | tf_op jit(solution)/shard_map/all_to_all | solution.py:755
  72.8 0.0 copy-done.1
  72.8 3.3 %solve.1 = (f32[128,128]{1,0:T(8,128)S(1)}, f32[53,8,8,256]{3,2,1,0:T(8,128)}) custom-call(f32[256]{0:T(256)S(1)} %copy-done.3, f32[128,128]{1,0:T(8,128)S(1)} %bitcast.11, f32[64,128]{1,0:T(8,128)S(1)} %copy-done.1, f32[256,256]{1,0:T(8,128)S(1)} %copy-done, f32[32,128]{1,0:T(8,128)S(1)} %copy-done.2, f32[10,2,448,128]{3,2,1,0:T(8,128)S(1)} %get-tuple-element.35.mv), custom_call_target="tpu_custom_call" | custom-call | tf_op jit(solution)/shard_map/solve/pallas_call | solution.py:767
  76.1 9.1 %all_to_all.11 = f32[32,4,128]{2,1,0:T(4,128)S(1)} all-to-all(f32[32,4,128]{2,1,0:T(4,128)S(1)} %bitcast.14), channel_id=1, replica_groups=mesh['row'=4,'col'=8] {'row','col'}, dimensions={0} | all-to-all | bytes 131072 | tf_op jit(solution)/shard_map/all_to_all | solution.py:755
  85.2 0.9 %inverse.1 = f32[64,256]{1,0:T(8,128)} custom-call(f32[128,128]{1,0:T(8,128)S(1)} %bitcast.12, bf16[256,256]{1,0:T(8,128)(2,1)S(1)} %get-tuple-element.38.table_high, bf16[256,256]{1,0:T(8,128)(2,1)S(1)} %get-tuple-element.39.table_low), custom_call_target="tpu_custom_call" | custom-call | tf_op jit(solution)/shard_map/inverse/pallas_call | solution.py:788
  (4 shorter events, 0.0 us)
Async XLA Ops:
  4.7 18.2 %collective-permute-start = (f32[53,8,256]{2,1,0:T(8,128)S(1)}, f32[53,8,256]{2,1,0:T(8,128)S(1)}, u32[]{:S(2)}, u32[]{:S(2)}) collective-permute-start(f32[53,8,256]{2,1,0:T(8,128)S(1)} %get-tuple-element.30.row_sent_a), channel_id=1, source_target_pairs={{0,8},{8,0},{16,24},{24,16},{1,9},{9,1},{17,25},{25,17},{2,10},{10... | collective-permute-start | bytes 1302536 | tf_op jit(solution)/shard_map/ppermute | solution.py:678
  7.8 15.1 %collective-permute-start.1 = (f32[53,8,256]{2,1,0:T(8,128)S(1)}, f32[53,8,256]{2,1,0:T(8,128)S(1)}, u32[]{:S(2)}, u32[]{:S(2)}) collective-permute-start(f32[53,8,256]{2,1,0:T(8,128)S(1)} %get-tuple-element.31.row_sent_b), channel_id=1, source_target_pairs={{8,16},{16,8},{9,17},{17,9},{10,18},{18,10},{11,19},{19,11},{12,20... | collective-permute-start | bytes 1302536 | tf_op jit(solution)/shard_map/ppermute | solution.py:678
  8.5 14.4 %collective-permute-start.2 = (f32[53,8,256]{2,1,0:T(8,128)S(1)}, f32[53,8,256]{2,1,0:T(8,128)S(1)}, u32[]{:S(2)}, u32[]{:S(2)}) collective-permute-start(f32[53,8,256]{2,1,0:T(8,128)S(1)} %get-tuple-element.32.col_sent_a), channel_id=1, source_target_pairs={{0,1},{1,0},{2,3},{3,2},{4,5},{5,4},{6,7},{7,6},{8,9},{9,8},{10,11... | collective-permute-start | bytes 1302536 | tf_op jit(solution)/shard_map/ppermute | solution.py:678
  8.6 14.3 %collective-permute-start.3 = (f32[53,8,256]{2,1,0:T(8,128)S(1)}, f32[53,8,256]{2,1,0:T(8,128)S(1)}, u32[]{:S(2)}, u32[]{:S(2)}) collective-permute-start(f32[53,8,256]{2,1,0:T(8,128)S(1)} %get-tuple-element.33.col_sent_b), channel_id=1, source_target_pairs={{1,2},{2,1},{3,4},{4,3},{5,6},{6,5},{9,10},{10,9},{11,12},{12,11},... | collective-permute-start | bytes 1302536 | tf_op jit(solution)/shard_map/ppermute | solution.py:678
  9.3 13.6 %copy-start.4 = (f32[8,8,256]{2,1,0:T(8,128)S(1)}, f32[8,8,256]{2,1,0:T(8,128)}, u32[]{:S(2)}) copy-start(f32[8,8,256]{2,1,0:T(8,128)} %param.18) | copy-start | bytes 196612
  9.3 13.6 %copy-start.5 = (f32[256,256]{1,0:T(8,128)S(1)}, f32[256,256]{1,0:T(8,128)}, u32[]{:S(2)}) copy-start(f32[256,256]{1,0:T(8,128)} %constant.13.clone.table_z) | copy-start | bytes 786436
  22.9 49.8 %copy-start = (f32[256,256]{1,0:T(8,128)S(1)}, f32[256,256]{1,0:T(8,128)}, u32[]{:S(2)}) copy-start(f32[256,256]{1,0:T(8,128)} %constant.16.clone.mix_x) | copy-start | bytes 786436
  22.9 49.8 %copy-start.1 = (f32[64,128]{1,0:T(8,128)S(1)}, f32[64,128]{1,0:T(8,128)}, u32[]{:S(2)}) copy-start(f32[64,128]{1,0:T(8,128)} %constant.15.clone.table_y) | copy-start | bytes 98308
  22.9 49.8 %copy-start.2 = (f32[32,128]{1,0:T(8,128)S(1)}, f32[32,128]{1,0:T(8,128)}, u32[]{:S(2)}) copy-start(f32[32,128]{1,0:T(8,128)} %constant.17.clone.base) | copy-start | bytes 49156
  23.0 49.8 %copy-start.3 = (f32[256]{0:T(256)S(1)}, f32[256]{0:T(256)}, u32[]{:S(2)}) copy-start(f32[256]{0:T(256)} %constant.14.clone.lam_z) | copy-start | bytes 3076

commit v2 on v1

--- a/solution.py
+++ b/solution.py
@@ -188,7 +188,7 @@
     small_sem,
 ):
     ns, cx, cy, halves_z = dims
-    nr = log_rates.shape[1]
+    nr = log_rates.shape[0]
     ns8 = weight_ref.shape[0]
 
     def load(x, z):
@@ -234,7 +234,7 @@
     build[...] = jnp.zeros_like(build)
     build[0:ns, 0:nr] = react
     build[ns8 : ns8 + ns, 0:nr] = react
-    rest = log_rates[...] * log2e
+    rest = log_rates[...].reshape(1, nr) * log2e
     for i in range(3):
         piece = rest.astype(bf16).astype(f32)
         build[ns + i : ns + i + 1, 0:nr] = piece
@@ -645,7 +645,7 @@
             pltpu.VMEM((ns, nr), jnp.int32),
             pltpu.VMEM((1, ns), f32),
             pltpu.VMEM(codes.shape, f32),
-            pltpu.VMEM((1, nr), f32),
+            pltpu.VMEM((nr,), f32),
             pltpu.VMEM((cx, halves_z, cy), jnp.int32),
             pltpu.VMEM((cx * halves_z, LANES), f32),
             pltpu.SemaphoreType.DMA((cx, halves_z)),
@@ -664,7 +664,7 @@
                 products.T,
                 heat_weights[None, :],
                 jnp.asarray(codes),
-                log_rates[None, :],
+                log_rates,
                 substeps.transpose(0, 2, 1),
             )
         ),

time: 85.8 us -> 78.6 us (0.916)
  blocking collectives: 44.3 us -> 31.1 us
  Pallas kernels: 35.1 us -> 42.4 us
  local copies, waits for them, and re-layouts: 1.29 us -> 0.04 us
    all_to_all x2, blocking collectives: 44.3 us -> 31.1 us  [exchange(): lax.all_to_all(value, ('row', 'col'), split_axis=0, concat_axis=0, tiled=...]
    pallas_call x1, Pallas kernels: 13.6 us -> 19.9 us  [local(): pl.pallas_call(functools.partial(inner_kernel, dims, inner_total, inner_g...]
    broadcast_in_dim x1 -> x0, local copies, waits for them, and re-layouts: 1.25 us -> none  [local(): log_rates[None, :]]
    pallas_call x1, Pallas kernels: 14.6 us -> 15.5 us  [local(): pl.pallas_call(functools.partial(outer_kernel, dims, inner_total, outer_t...]
  transfers between devices with their start and end apart: 4 -> 4, of which waited for: 0 -> 0; matrix products, arithmetic and copies ran while one was open for 0% -> 0% of each run, Pallas kernels for 16% -> 25%
where the time goes in v2:
time: 78.6 us; the launch traced here: 78.9 us
  Pallas kernels  42.4 us (54%)
  blocking collectives  31.1 us (40%)
  starting transfers between devices  4.55 us (6%)
  between operations  0.79 us (1%)
    all_to_all x2, blocking collectives, exchange(): lax.all_to_all(value, ('row', 'col'), split_axis=0, concat_axis=0, tiled=...  31.1 us
    pallas_call x1, Pallas kernels, local(): pl.pallas_call(functools.partial(inner_kernel, dims, inner_total, inner_g...  19.9 us
    pallas_call x1, Pallas kernels, local(): pl.pallas_call(functools.partial(outer_kernel, dims, inner_total, outer_t...  15.5 us
    ppermute x4, starting transfers between devices, swap(): return lax.ppermute(value, axis, pairs)  4.55 us
    pallas_call x1, Pallas kernels, solve(): pl.pallas_call(functools.partial(solve_kernel, dims), out_shape=(jax.Shap...  3.3 us
    pallas_call x1, Pallas kernels, local(): pl.pallas_call(functools.partial(prepare_kernel, dims), out_shape=(array(...  2.82 us
  transfers between devices with their start and end apart: 4, of which 0 were waited for; matrix products, arithmetic and copies ran while one was open for 0% of the time, Pallas kernels for 25%

profile of v2, /device:TPU:0, one launch (start us, length us, event | category | flops | bytes accessed | tf_op | source)
XLA Modules:
  0.0 78.9 jit_solution(1226488489560331960)
XLA Ops:
  0.6 2.8 %prepare.1 = (f32[2,53,8,8,128]{4,3,2,1,0:T(8,128)S(1)}, f32[53,8,256]{2,1,0:T(8,128)S(1)}, f32[53,8,256]{2,1,0:T(8,128)S(1)}, f32[53,8,256]{2,1,0:T(8,128)S(1)}...) custom-call(f32[53,8,8,256]{3,2,1,0:T(8,128)} %species_hbm.1, ...), custom_call_target="tpu_custom_call" | custom-call | tf_op jit(solution)/shard_map/prepare/pallas_call | solution.py:628
  3.5 3.1 %collective-permute-start = (f32[53,8,256]{2,1,0:T(8,128)S(1)}, f32[53,8,256]{2,1,0:T(8,128)S(1)}, u32[]{:S(2)}, u32[]{:S(2)}) collective-permute-start(f32[53,8,256]{2,1,0:T(8,128)S(1)} %get-tuple-element.30.row_sent_a), channel_id=1, source_target_pairs={{0,8},{8,0},{16,24},{24,16},{1,9},{9,1},{17,25},{25,17},{2,10},{10... | collective-permute-start | bytes 1302536 | tf_op jit(solution)/shard_map/ppermute | solution.py:678
  6.6 0.7 collective-permute-start.1
  7.3 0.1 collective-permute-start.2
  7.3 0.7 collective-permute-start.3
  8.0 0.0 copy-start.4
  8.0 0.0 copy-start.5
  8.1 19.9 %inner.1 = (f32[10,2,448,128]{3,2,1,0:T(8,128)S(1)}, f32[2,64,128]{2,1,0:T(8,128)S(1)}) custom-call(s32[1,128]{1,0:T(1,128)S(1)} %get-tuple-element.21.order, f32[1,53]{1,0:T(1,128)S(1)} %get-tuple-element.22.diffusivity, f32[2,53,8,8,128]{4,3,2,1,0:T(8,128)S(1)} %get-tuple-element.24.sp, f32[3,8,8,256]{3,2,1,0:T(8,128)S(1)} %get-tuple-element.23.velocity, ...), custom_call_target="tpu_custom_call" | custom-call | flops 10000000000 | bytes 10000000 | tf_op jit(solution)/shard_map/inner/pallas_call | solution.py:684
  28.0 0.0 collective-permute-done.row_got_a
  28.0 0.0 collective-permute-done.1.row_got_b
  28.0 0.0 collective-permute-done.2.col_got_a
  28.0 0.0 collective-permute-done.3.col_got_b
  28.0 0.0 copy-done.4
  28.0 0.0 copy-start
  28.1 0.0 copy-start.1
  28.1 0.0 copy-start.2
  28.1 0.0 copy-start.3
  28.1 15.5 %outer.1 = (f32[128,128]{1,0:T(8,128)S(1)}, f32[10,2,448,128]{3,2,1,0:T(8,128)S(1)}, bf16[256,256]{1,0:T(8,128)(2,1)S(1)}, bf16[256,256]{1,0:T(8,128)(2,1)S(1)}) custom-call(s32[1,128]{1,0:T(1,128)S(1)} %get-tuple-element.21.order, f32[1,53]{1,0:T(1,128)S(1)} %get-tuple-element.22.diffusivity, ...), custom_call_target="tpu_custom_call", output_to_operand_aliasing={{1}: (4, {})} | custom-call | flops 10000000000 | bytes 10000000 | tf_op jit(solution)/shard_map/outer/pallas_call | solution.py:701
  43.6 22.0 %all_to_all.10 = f32[32,4,128]{2,1,0:T(4,128)S(1)} all-to-all(f32[32,4,128]{2,1,0:T(4,128)S(1)} %bitcast.13), channel_id=1, replica_groups=mesh['row'=4,'col'=8] {'row','col'}, dimensions={0} | all-to-all | bytes 131072 | tf_op jit(solution)/shard_map/all_to_all | solution.py:755
  65.6 0.0 copy-done.2
  65.6 0.0 copy-done.3
  65.6 3.3 %solve.1 = (f32[128,128]{1,0:T(8,128)S(1)}, f32[53,8,8,256]{3,2,1,0:T(8,128)}) custom-call(f32[256]{0:T(256)S(1)} %copy-done.3, f32[128,128]{1,0:T(8,128)S(1)} %bitcast.11, f32[64,128]{1,0:T(8,128)S(1)} %copy-done.1, f32[256,256]{1,0:T(8,128)S(1)} %copy-done, f32[32,128]{1,0:T(8,128)S(1)} %copy-done.2, f32[10,2,448,128]{3,2,1,0:T(8,128)S(1)} %get-tuple-element.35.mv), custom_call_target="tpu_custom_call" | custom-call | tf_op jit(solution)/shard_map/solve/pallas_call | solution.py:767
  68.9 9.1 %all_to_all.11 = f32[32,4,128]{2,1,0:T(4,128)S(1)} all-to-all(f32[32,4,128]{2,1,0:T(4,128)S(1)} %bitcast.14), channel_id=1, replica_groups=mesh['row'=4,'col'=8] {'row','col'}, dimensions={0} | all-to-all | bytes 131072 | tf_op jit(solution)/shard_map/all_to_all | solution.py:755
  78.0 0.9 %inverse.1 = f32[64,256]{1,0:T(8,128)} custom-call(f32[128,128]{1,0:T(8,128)S(1)} %bitcast.12, bf16[256,256]{1,0:T(8,128)(2,1)S(1)} %get-tuple-element.38.table_high, bf16[256,256]{1,0:T(8,128)(2,1)S(1)} %get-tuple-element.39.table_low), custom_call_target="tpu_custom_call" | custom-call | tf_op jit(solution)/shard_map/inverse/pallas_call | solution.py:788
  (3 shorter events, 0.0 us)
Async XLA Ops:
  3.5 24.5 %collective-permute-start = (f32[53,8,256]{2,1,0:T(8,128)S(1)}, f32[53,8,256]{2,1,0:T(8,128)S(1)}, u32[]{:S(2)}, u32[]{:S(2)}) collective-permute-start(f32[53,8,256]{2,1,0:T(8,128)S(1)} %get-tuple-element.30.row_sent_a), channel_id=1, source_target_pairs={{0,8},{8,0},{16,24},{24,16},{1,9},{9,1},{17,25},{25,17},{2,10},{10... | collective-permute-start | bytes 1302536 | tf_op jit(solution)/shard_map/ppermute | solution.py:678
  6.6 21.4 %collective-permute-start.1 = (f32[53,8,256]{2,1,0:T(8,128)S(1)}, f32[53,8,256]{2,1,0:T(8,128)S(1)}, u32[]{:S(2)}, u32[]{:S(2)}) collective-permute-start(f32[53,8,256]{2,1,0:T(8,128)S(1)} %get-tuple-element.31.row_sent_b), channel_id=1, source_target_pairs={{8,16},{16,8},{9,17},{17,9},{10,18},{18,10},{11,19},{19,11},{12,20... | collective-permute-start | bytes 1302536 | tf_op jit(solution)/shard_map/ppermute | solution.py:678
  7.3 20.7 %collective-permute-start.2 = (f32[53,8,256]{2,1,0:T(8,128)S(1)}, f32[53,8,256]{2,1,0:T(8,128)S(1)}, u32[]{:S(2)}, u32[]{:S(2)}) collective-permute-start(f32[53,8,256]{2,1,0:T(8,128)S(1)} %get-tuple-element.32.col_sent_a), channel_id=1, source_target_pairs={{0,1},{1,0},{2,3},{3,2},{4,5},{5,4},{6,7},{7,6},{8,9},{9,8},{10,11... | collective-permute-start | bytes 1302536 | tf_op jit(solution)/shard_map/ppermute | solution.py:678
  7.3 20.7 %collective-permute-start.3 = (f32[53,8,256]{2,1,0:T(8,128)S(1)}, f32[53,8,256]{2,1,0:T(8,128)S(1)}, u32[]{:S(2)}, u32[]{:S(2)}) collective-permute-start(f32[53,8,256]{2,1,0:T(8,128)S(1)} %get-tuple-element.33.col_sent_b), channel_id=1, source_target_pairs={{1,2},{2,1},{3,4},{4,3},{5,6},{6,5},{9,10},{10,9},{11,12},{12,11},... | collective-permute-start | bytes 1302536 | tf_op jit(solution)/shard_map/ppermute | solution.py:678
  8.0 20.0 %copy-start.4 = (f32[8,8,256]{2,1,0:T(8,128)S(1)}, f32[8,8,256]{2,1,0:T(8,128)}, u32[]{:S(2)}) copy-start(f32[8,8,256]{2,1,0:T(8,128)} %param.18) | copy-start | bytes 196612
  8.0 20.0 %copy-start.5 = (f32[256,256]{1,0:T(8,128)S(1)}, f32[256,256]{1,0:T(8,128)}, u32[]{:S(2)}) copy-start(f32[256,256]{1,0:T(8,128)} %constant.13.clone.table_z) | copy-start | bytes 786436
  28.0 37.5 %copy-start = (f32[256,256]{1,0:T(8,128)S(1)}, f32[256,256]{1,0:T(8,128)}, u32[]{:S(2)}) copy-start(f32[256,256]{1,0:T(8,128)} %constant.16.clone.mix_x) | copy-start | bytes 786436
  28.1 37.5 %copy-start.1 = (f32[64,128]{1,0:T(8,128)S(1)}, f32[64,128]{1,0:T(8,128)}, u32[]{:S(2)}) copy-start(f32[64,128]{1,0:T(8,128)} %constant.15.clone.table_y) | copy-start | bytes 98308
  28.1 37.5 %copy-start.2 = (f32[32,128]{1,0:T(8,128)S(1)}, f32[32,128]{1,0:T(8,128)}, u32[]{:S(2)}) copy-start(f32[32,128]{1,0:T(8,128)} %constant.17.clone.base) | copy-start | bytes 49156
  28.1 37.5 %copy-start.3 = (f32[256]{0:T(256)S(1)}, f32[256]{0:T(256)}, u32[]{:S(2)}) copy-start(f32[256]{0:T(256)} %constant.14.clone.lam_z) | copy-start | bytes 3076
